TPU v7x, 512 devices: a whole 4x4x16 slice. The times are simulated.
512 devices in a mesh: wide: 128 (over z, y, core), narrow: 4 (over x).
Axes of the slice: x: 4, y: 4, z: 16, core: 2. Of those that a mesh axis runs over, the one named last changes fastest.
Arguments:
- tokens: bfloat16 [1024, 1024], P('wide', 'narrow'), may hold values from -6 to 6
- norm_gain: float32 [1024], replicated, may hold values from 0.1 to 1.9
- w_qk: bfloat16 [1024, 2, 1024], P(None, None, 'narrow'), may hold values from -0.0625 to 0.0625
- w_value: bfloat16 [1024, 1024], P(None, 'narrow'), may hold values from -0.1875 to 0.1875
- w_out: bfloat16 [1024, 1024], P('narrow'), may hold values from -1.5 to 1.5
- kv_cache: bfloat16 [8192, 2, 32, 1024], P('wide', None, None, 'narrow'), may hold values from -200 to 200
- cache_len: int32 [1024], replicated, may hold values from 1 to 256, as said below
- page_table: int32 [1024, 8], replicated, may hold values from 0 to 63, as said below
Outputs:
- attended: bfloat16 [1024, 1024], P('wide', 'narrow')
Inputs may be any that keep to these rules, and one draw needn't show every extreme that they name: `cache_len`: every request has one or more cached positions, and some request has exactly 256. `page_table`: on every owner, the pairs (request, page) placed there by the rule of the steps occupy its 64 slots one to one.
All inputs are finite; a program needn't handle non-finite values.
Results may differ from a plain program's by a relative error of at most 0.015.
The roundings to bfloat16 on the way count: a program that leaves them out, or rounds other values in their place, can miss the bound.
Values may be sent and summed in bfloat16 or wider, within the bound.
A program may use at most 64 MiB of HBM per device.

v0:
```python
import jax
import jax.numpy as jnp
from jax import lax
from jax.sharding import PartitionSpec as P

HEAD_DIM = 64


def page_partial(query_rows, request_rows, page_rows, kv_cache, cache_len, page_table):
    count = query_rows.shape[0]
    width = query_rows.shape[1]
    local_heads = width // HEAD_DIM
    page_len = kv_cache.shape[2]
    slot_rows = page_table[request_rows, page_rows]
    lengths = cache_len[request_rows]
    keys = kv_cache[slot_rows, 0].reshape(count, page_len, local_heads, HEAD_DIM)
    values = kv_cache[slot_rows, 1].reshape(count, page_len, local_heads, HEAD_DIM)
    q_heads = query_rows.reshape(count, local_heads, HEAD_DIM)
    scores = jnp.einsum("nhe,nphe->nhp", q_heads, keys, preferred_element_type=jnp.float32)
    places = page_rows[:, None] * page_len + jnp.arange(page_len, dtype=jnp.int32)[None, :]
    valid = (places < lengths[:, None])[:, None, :]
    scores = jnp.where(valid, scores, -1e30)
    page_max = jnp.max(scores, axis=-1)
    weights = jnp.where(valid, jnp.exp(scores - page_max[..., None]), 0.0)
    page_sum = jnp.sum(weights, axis=-1)
    page_acc = jnp.einsum(
        "nhp,nphe->nhe", weights.astype(jnp.bfloat16), values, preferred_element_type=jnp.float32
    )
    return (page_max, page_sum, page_acc.reshape(count, width))


def body(tokens, norm_gain, w_qk, w_value, w_out, kv_cache, cache_len, page_table):
    gathered = lax.all_gather(tokens, "narrow", axis=1, tiled=True)
    floats = gathered.astype(jnp.float32)
    normed = (
        floats * lax.rsqrt(jnp.mean(floats * floats, axis=-1, keepdims=True) + 1e-06) * norm_gain
    ).astype(jnp.bfloat16)
    both = jnp.einsum("td,dcf->tcf", normed, w_qk, preferred_element_type=jnp.float32).astype(
        jnp.bfloat16
    )
    own_queries = both[:, 0, :]
    new_keys = both[:, 1, :]
    new_values = jnp.dot(normed, w_value, preferred_element_type=jnp.float32).astype(jnp.bfloat16)
    tok_count = tokens.shape[0]
    width = own_queries.shape[1]
    local_heads = width // HEAD_DIM
    page_count = page_table.shape[1]
    wide_count = lax.axis_size("wide")
    stride_len = wide_count // page_count
    my_index = lax.axis_index("wide")
    local_ids = jnp.arange(tok_count, dtype=jnp.int32)
    self_score = jnp.sum(
        own_queries.reshape(tok_count, local_heads, HEAD_DIM).astype(jnp.float32)
        * new_keys.reshape(tok_count, local_heads, HEAD_DIM).astype(jnp.float32),
        axis=-1,
    )
    value_heads = new_values.reshape(tok_count, local_heads, HEAD_DIM).astype(jnp.float32)
    all_queries = lax.all_gather(own_queries, "wide", axis=0, tiled=True)
    page_rows = jnp.repeat(jnp.arange(page_count, dtype=jnp.int32), tok_count)
    slot_local = jnp.tile(local_ids, page_count)
    page_offsets = (page_rows - page_rows % 2) * stride_len + page_rows % 2
    home_rows = (my_index - page_offsets) % wide_count
    request_rows = home_rows * tok_count + slot_local
    page_max, page_sum, page_acc = page_partial(
        all_queries[request_rows], request_rows, page_rows, kv_cache, cache_len, page_table
    )
    total = wide_count * tok_count
    max_table = jnp.full((total, local_heads), -1e30, jnp.float32).at[request_rows].set(page_max)
    best = lax.pmax(max_table, "wide")
    factor = jnp.exp(page_max - best[request_rows])
    scaled = (page_acc.reshape(-1, local_heads, HEAD_DIM) * factor[..., None]).reshape(-1, width)
    numer_table = jnp.zeros((total, width), jnp.float32).at[request_rows].set(scaled)
    denom_table = (
        jnp.zeros((total, local_heads), jnp.float32).at[request_rows].set(page_sum * factor)
    )
    numer, denom = (
        lax.psum_scatter(numer_table, "wide", scatter_dimension=0, tiled=True),
        lax.psum_scatter(denom_table, "wide", scatter_dimension=0, tiled=True),
    )
    best_home = lax.dynamic_slice_in_dim(best, my_index * tok_count, tok_count, 0)
    top = jnp.maximum(best_home, self_score)
    rescale = jnp.exp(best_home - top)
    self_factor = jnp.exp(self_score - top)
    numer = (
        numer.reshape(tok_count, local_heads, HEAD_DIM) * rescale[..., None]
        + self_factor[..., None] * value_heads
    )
    denom = denom * rescale + self_factor
    heads_out = (numer / denom[..., None]).reshape(tok_count, width).astype(jnp.bfloat16)
    partial_out = jnp.dot(heads_out, w_out, preferred_element_type=jnp.float32)
    return lax.psum_scatter(partial_out, "narrow", scatter_dimension=1, tiled=True).astype(
        jnp.bfloat16
    )


def solution(mesh):
    placed = (
        P("wide", "narrow"),
        P(),
        P(None, None, "narrow"),
        P(None, "narrow"),
        P("narrow", None),
        P("wide", None, None, "narrow"),
        P(),
        P(),
    )
    return jax.shard_map(
        body, mesh=mesh, in_specs=placed, out_specs=P("wide", "narrow"), check_vma=False
    )
```

profile of v0, /device:TPU:1, one launch (start us, length us, event | category | flops | bytes accessed | tf_op | source)
XLA Modules:
  0.0 1147.7 jit_solution(1433137674564910092)
XLA Ops:
  6.6 0.1 reshape.245
  6.6 0.1 tile.10
  6.7 10.5 all_gather.6
  17.2 0.1 fusion.20
  17.3 1.5 convolution_convert_fusion
  18.9 93.3 %all-gather = bf16[1024,1,256]{2,0,1:T(8,128)(2,1)S(1)} all-gather(bf16[8,1,256]{2,0,1:T(8,128)(2,1)S(1)} %slice.20), channel_id=2, replica_groups=mesh['wide'=128,'narrow'=4] {'wide'}, dimensions={0}, use_global_device_ids=true | all-gather | bytes 528384 | tf_op jit(solution)/shard_map/all_gather | solution.py:58
  112.2 0.7 gather_fusion.1
  112.9 0.1 reshape.323
  113.0 0.8 gather_fusion.2
  113.8 0.7 gather_fusion.3
  114.5 1.9 reshape.247
  116.5 2.8 fusion.2
  119.3 0.1 copy.27
  119.3 0.0 copy-done.1
  119.4 0.7 gather_fusion
  120.1 0.1 mul.110
  120.3 0.1 copy.21
  120.4 0.9 scatter_custom_fusion
  121.2 488.0 %pmax.7 = f32[1024,4]{1,0:T(8,128)S(1)} all-reduce(f32[1024,4]{1,0:T(8,128)S(1)} %scatter_custom_fusion), channel_id=1, replica_groups=mesh['wide'=128,'narrow'=4] {'wide'}, use_global_device_ids=true, to_apply=%region_3.4 | all-reduce | flops 4096 | bytes 32768 | tf_op jit(solution)/shard_map/pmax | solution.py:69
  609.2 0.6 gather_fusion.5
  609.8 0.1 copy.22
  609.9 0.1 copy.28
  610.1 0.7 gather_fusion.4
  610.8 1.9 reshape.248
  612.7 0.1 copy.23
  612.8 2.2 fusion
  615.0 0.1 broadcast_multiply_fusion
  615.2 0.1 reshape.304
  615.3 1.8 scatter_custom_fusion.1
  617.1 0.0 reduce-scatter.3.cloned.1.call-update
  617.1 0.0 reduce-scatter.5.cloned.1.call-start
  617.2 0.1 copy.24
  617.3 0.9 scatter_custom_fusion.2
  618.2 0.1 mul.120
  618.3 0.1 reduce_sum.28
  618.4 1.3 dynamic-slice
  620.3 491.0 %all-reduce.2 = f32[1024,4]{1,0:T(8,128)S(1)} all-reduce(f32[1024,4]{1,0:T(8,128)S(1)} %scatter_custom_fusion.2), channel_id=4, replica_groups=mesh['wide'=128,'narrow'=4] {'wide'}, use_global_device_ids=true, to_apply=%region_9.10.clone | all-reduce | flops 4096 | bytes 32768
  1111.2 0.7 fusion.28
  1111.9 0.1 div.15
  1112.0 0.1 div.16
  1112.1 0.1 mul.124
  1112.1 0.1 mul.125
  1112.2 0.1 mul.121
  1112.3 0.1 mul.122
  1112.4 2.3 fusion.9
  1114.7 0.0 reduce-scatter.5.cloned.1.call-update
  1114.8 24.8 %reduce-scatter.5.cloned.1.call-done = f32[8,256]{1,0:T(8,128)} async-done(((f32[8,1024]{1,0:T(8,128)}), f32[8,256]{1,0:T(8,128)}) %reduce-scatter.5.cloned.1.call-update) | async-done | bytes 8208 | tf_op jit(solution)/shard_map/reduce_scatter | solution.py:91
  1139.6 1.3 convert_element_type.50
  (24 shorter events, 0.2 us)
Async XLA Ops:
  6.5 107.3 %copy-start = (bf16[64,2,32,256]{3,2,1,0:T(8,128)(2,1)S(1)}, bf16[64,2,32,256]{3,2,1,0:T(8,128)(2,1)}, u32[]{:S(2)}) copy-start(bf16[64,2,32,256]{3,2,1,0:T(8,128)(2,1)} %param.13) | copy-start | bytes 6291460
  6.5 106.5 %copy-start.2 = (s32[1024,8]{0,1:T(8,128)S(1)}, s32[1024,8]{0,1:T(8,128)}, u32[]{:S(2)}) copy-start(s32[1024,8]{0,1:T(8,128)} %param.15) | copy-start | bytes 98308
  6.5 1105.9 %reduce-scatter.3.cloned.1.call-start = ((), (), s32[]{:S(2)}) async-start(), calls=%async_computation.2 | async-start | bytes 1056768 | tf_op jit(solution)/shard_map/reduce_scatter | solution.py:77
  116.5 2.9 copy-start.1
  609.2 0.8 copy-start.3
  615.2 497.2 %copy-start.4 = (f32[1024]{0:T(1024)S(1)}, f32[1024]{0:T(1024)}, u32[]{:S(2)}) copy-start(f32[1024]{0:T(1024)} %param.9) | copy-start | bytes 12292
  617.1 522.4 %reduce-scatter.5.cloned.1.call-start = ((), (), s32[]{:S(2)}) async-start(), calls=%async_computation.3 | async-start | bytes 40960 | tf_op jit(solution)/shard_map/reduce_scatter | solution.py:91
Sparse Core Ops, SparseCore 0:
  617.3 249.4 reduce-scatter.2
  1114.9 24.6 reduce-scatter.4
where the time goes:
time: 1150 us
  blocking collectives  1080 us (94%)
  waiting for transfers between devices  24.9 us (2%)
  local copies, waits for them, and re-layouts  14.5 us (1%)
  between operations  14.2 us (1%)
    unnamed x1, blocking collectives  491 us
    pmax x1, blocking collectives, body(): best = lax.pmax(max_table, 'wide')  488 us
    all_gather x1, blocking collectives, body(): all_queries = lax.all_gather(own_queries, 'wide', axis=0, tiled=True)  93.3 us
    reduce_scatter x1, waiting for transfers between devices, body(): lax.psum_scatter(partial_out, 'narrow', scatter_dimension=1, tiled=True)  24.8 us
  transfers between devices with their start and end apart: 2, of which 1 were waited for; matrix products, arithmetic and copies ran while one was open for 0% of the time, Pallas kernels for 0%

commit v1 on v0

v1 whole, which is shorter than its diff:
```python
import functools

import jax
import jax.numpy as jnp
from jax import lax
from jax.experimental import pallas as pl
from jax.experimental.pallas import tpu as pltpu
from jax.sharding import PartitionSpec as P

HEAD_DIM = 64
MESH = pl.DeviceIdType.MESH
NEG = -1e30


def layer_kernel(
    wide, narrow, offs,
    tok, gain, wqk, wv, wo, kv, clen, ptab, out,
    tokb, gainb, wqkb, wvb, wob, kvb, lenb, ptb, qin, pout, pin, rsout, rsin,
    lsem, tsend, trecv, qsend, qrecv, psend, precv, rsend, rrecv,
):
    me_w = lax.axis_index("wide")
    me_x = lax.axis_index("narrow")
    tcount, width = tok.shape
    pages = len(offs)
    heads = width // HEAD_DIM
    page_len = kvb.shape[2]
    span = tcount * page_len

    def fwd(j):
        return lax.rem(me_w + offs[j], wide)

    def bwd(j):
        return lax.rem(me_w + (wide - offs[j]), wide)

    local = [
        pltpu.make_async_copy(tok, tokb.at[me_x], lsem.at[0]),
        pltpu.make_async_copy(gain, gainb, lsem.at[1]),
        pltpu.make_async_copy(wqk, wqkb, lsem.at[2]),
        pltpu.make_async_copy(wv, wvb, lsem.at[3]),
        pltpu.make_async_copy(clen, lenb, lsem.at[4]),
        pltpu.make_async_copy(ptab, ptb, lsem.at[5]),
        pltpu.make_async_copy(kv, kvb, lsem.at[6]),
        pltpu.make_async_copy(wo, wob, lsem.at[7]),
    ]
    for copy in local:
        copy.start()

    around = sorted({o for o in offs if o} | {wide - o for o in offs if o})
    barrier = pltpu.get_barrier_semaphore()
    for d in range(1, narrow):
        pl.semaphore_signal(
            barrier, inc=1, device_id=(me_w, lax.rem(me_x + d, narrow)), device_id_type=MESH
        )
    for o in around:
        pl.semaphore_signal(
            barrier, inc=1, device_id=(lax.rem(me_w + o, wide), me_x), device_id_type=MESH
        )
    pl.semaphore_wait(barrier, narrow - 1 + len(around))

    tcopies = [
        pltpu.make_async_remote_copy(
            src_ref=tok, dst_ref=tokb.at[me_x], send_sem=tsend.at[d - 1], recv_sem=trecv.at[d - 1],
            device_id=(me_w, lax.rem(me_x + d, narrow)), device_id_type=MESH,
        )
        for d in range(1, narrow)
    ]
    for copy in tcopies:
        copy.start()
    local[0].wait()
    local[1].wait()
    for copy in tcopies:
        copy.wait_recv()

    floats = [tokb[i].astype(jnp.float32) for i in range(narrow)]
    square = functools.reduce(
        jnp.add, [jnp.sum(f * f, axis=-1, keepdims=True) for f in floats]
    )
    scale = lax.rsqrt(square / (narrow * width) + 1e-06)
    normed = [
        (floats[i] * scale * gainb[:, i * width:(i + 1) * width]).astype(jnp.bfloat16)
        for i in range(narrow)
    ]

    local[2].wait()

    def project(weight):
        return functools.reduce(
            jnp.add,
            [
                jnp.dot(
                    normed[i], weight(i * width, (i + 1) * width),
                    preferred_element_type=jnp.float32,
                )
                for i in range(narrow)
            ],
        ).astype(jnp.bfloat16)

    query = project(lambda a, b: wqkb[a:b, 0, :])
    qin[0] = query
    qcopies = {
        j: pltpu.make_async_remote_copy(
            src_ref=qin.at[0], dst_ref=qin.at[j], send_sem=qsend.at[j], recv_sem=qrecv.at[j],
            device_id=(fwd(j), me_x), device_id_type=MESH,
        )
        for j in range(1, pages)
    }
    far = sorted(range(1, pages), key=lambda j: -min(offs[j], wide - offs[j]))
    for j in far:
        qcopies[j].start()

    new_keys = project(lambda a, b: wqkb[a:b, 1, :]).astype(jnp.float32)
    local[3].wait()
    new_values = project(lambda a, b: wvb[a:b, :]).astype(jnp.float32)
    products = query.astype(jnp.float32) * new_keys
    lane = lax.broadcasted_iota(jnp.int32, (tcount, 128), 1)
    head_of = lax.broadcasted_iota(jnp.int32, (tcount, width), 1) // HEAD_DIM

    def stat_tile(columns, base, start):
        tile = start
        for h, column in enumerate(columns):
            tile = jnp.where(lane == base + h, column, tile)
        return tile

    self_score = stat_tile(
        [
            jnp.sum(jnp.where(head_of == h, products, 0.0), axis=-1, keepdims=True)
            for h in range(heads)
        ],
        0, jnp.full((tcount, 128), NEG, jnp.float32),
    )

    local[4].wait()
    local[5].wait()
    local[6].wait()
    row = lax.broadcasted_iota(jnp.int32, (tcount, span), 0)
    place = lax.broadcasted_iota(jnp.int32, (tcount, span), 1) - row * page_len

    def attend(j):
        home = bwd(j) * tcount
        q = qin[j].astype(jnp.float32)
        spread = jnp.concatenate(
            [jnp.where(head_of == h, q, 0.0) for h in range(heads)], axis=0
        ).astype(jnp.bfloat16)
        slots = [ptb[j, home + r] for r in range(tcount)]
        keys = jnp.concatenate([kvb[s, 0] for s in slots], axis=0)
        values = jnp.concatenate([kvb[s, 1] for s in slots], axis=0)
        limit = jnp.full((tcount, span), 0, jnp.int32)
        for r in range(tcount):
            limit = jnp.where(
                row == r, jnp.minimum(lenb[home + r] - j * page_len, page_len), limit
            )
        valid1 = (place >= 0) & (place < limit)
        valid = jnp.concatenate([valid1] * heads, axis=0)
        scores = lax.dot_general(
            spread, keys, (((1,), (1,)), ((), ())), preferred_element_type=jnp.float32
        )
        scores = jnp.where(valid, scores, NEG)
        top = jnp.max(scores, axis=-1, keepdims=True)
        weights = jnp.where(valid, jnp.exp(scores - top), 0.0)
        total = jnp.sum(weights, axis=-1, keepdims=True)
        acc = jnp.dot(weights.astype(jnp.bfloat16), values, preferred_element_type=jnp.float32)
        mine = jnp.zeros((tcount, width), jnp.float32)
        for h in range(heads):
            mine = jnp.where(head_of == h, acc[h * tcount:(h + 1) * tcount], mine)
        stats = stat_tile(
            [top[h * tcount:(h + 1) * tcount] for h in range(heads)],
            0, jnp.full((tcount, 128), 0.0, jnp.float32),
        )
        stats = stat_tile(
            [total[h * tcount:(h + 1) * tcount] for h in range(heads)], 64, stats
        )
        return mine, stats

    pcopies = {
        j: pltpu.make_async_remote_copy(
            src_ref=pout.at[j], dst_ref=pin.at[j], send_sem=psend.at[j], recv_sem=precv.at[j],
            device_id=(bwd(j), me_x), device_id_type=MESH,
        )
        for j in range(1, pages)
    }
    mine, stats = attend(0)
    pin[0, :, :width] = mine
    pin[0, :, width:] = stats
    for j in reversed(far):
        qcopies[j].wait_recv()
        mine, stats = attend(j)
        pout[j, :, :width] = mine
        pout[j, :, width:] = stats
        pcopies[j].start()

    for j in reversed(far):
        pcopies[j].wait_recv()

    stats = [pin[j, :, width:] for j in range(pages)]
    best = functools.reduce(jnp.maximum, stats, self_score)
    self_factor = jnp.exp(self_score - best)
    factors = [jnp.exp(s - best) for s in stats]
    denom = self_factor
    for j in range(pages):
        denom = denom + factors[j] * pltpu.roll(stats[j], 64, 1)

    def widen(tile):
        wide_tile = jnp.zeros((tcount, width), jnp.float32)
        for h in range(heads):
            wide_tile = jnp.where(head_of == h, tile[:, h:h + 1], wide_tile)
        return wide_tile

    numer = widen(self_factor) * new_values
    for j in range(pages):
        numer = numer + widen(factors[j]) * pin[j, :, :width]
    heads_out = (numer / widen(denom)).astype(jnp.bfloat16)

    local[7].wait()
    rcopies = []
    for d in range(1, narrow):
        peer = lax.rem(me_x + d, narrow)
        start = pl.multiple_of(peer * width, width)
        rsout[d - 1] = jnp.dot(
            heads_out, wob[:, pl.ds(start, width)], preferred_element_type=jnp.float32
        )
        copy = pltpu.make_async_remote_copy(
            src_ref=rsout.at[d - 1], dst_ref=rsin.at[d - 1],
            send_sem=rsend.at[d - 1], recv_sem=rrecv.at[d - 1],
            device_id=(me_w, peer), device_id_type=MESH,
        )
        copy.start()
        rcopies.append(copy)
    start = pl.multiple_of(me_x * width, width)
    total = jnp.dot(heads_out, wob[:, pl.ds(start, width)], preferred_element_type=jnp.float32)
    for d in range(1, narrow):
        rcopies[d - 1].wait_recv()
        total = total + rsin[d - 1]
    out[...] = total.astype(out.dtype)
    for copy in tcopies + rcopies + [qcopies[j] for j in far] + [pcopies[j] for j in far]:
        copy.wait_send()


def body(wide, narrow, tokens, norm_gain, w_qk, w_value, w_out, kv_cache, cache_len, page_table):
    tcount, width = tokens.shape
    total, pages = page_table.shape
    features = norm_gain.shape[0]
    stride_len = wide // pages
    offs = tuple(((j - j % 2) * stride_len + j % 2) % wide for j in range(pages))
    anywhere = pl.BlockSpec(memory_space=pl.ANY)
    dma = pltpu.SemaphoreType.DMA
    return pl.pallas_call(
        functools.partial(layer_kernel, wide, narrow, offs),
        out_shape=jax.ShapeDtypeStruct((tcount, width), jnp.bfloat16),
        in_specs=[anywhere] * 8,
        out_specs=pl.BlockSpec(memory_space=pltpu.VMEM),
        scratch_shapes=[
            pltpu.VMEM((narrow, tcount, width), jnp.bfloat16),
            pltpu.VMEM((1, features), jnp.float32),
            pltpu.VMEM(w_qk.shape, jnp.bfloat16),
            pltpu.VMEM(w_value.shape, jnp.bfloat16),
            pltpu.VMEM(w_out.shape, jnp.bfloat16),
            pltpu.VMEM(kv_cache.shape, jnp.bfloat16),
            pltpu.SMEM((total,), jnp.int32),
            pltpu.SMEM((pages, total), jnp.int32),
            pltpu.VMEM((pages, tcount, width), jnp.bfloat16),
            pltpu.VMEM((pages, tcount, width + 128), jnp.float32),
            pltpu.VMEM((pages, tcount, width + 128), jnp.float32),
            pltpu.VMEM((narrow - 1, tcount, width), jnp.float32),
            pltpu.VMEM((narrow - 1, tcount, width), jnp.float32),
            dma((8,)),
            dma((narrow - 1,)), dma((narrow - 1,)),
            dma((pages,)), dma((pages,)),
            dma((pages,)), dma((pages,)),
            dma((narrow - 1,)), dma((narrow - 1,)),
        ],
        compiler_params=pltpu.CompilerParams(
            collective_id=0, has_side_effects=True, vmem_limit_bytes=62 << 20
        ),
    )(
        tokens, norm_gain.reshape(1, features), w_qk, w_value, w_out, kv_cache, cache_len,
        page_table.T,
    )


def solution(mesh):
    placed = (
        P("wide", "narrow"),
        P(),
        P(None, None, "narrow"),
        P(None, "narrow"),
        P("narrow", None),
        P("wide", None, None, "narrow"),
        P(),
        P(),
    )
    return jax.shard_map(
        functools.partial(body, mesh.shape["wide"], mesh.shape["narrow"]),
        mesh=mesh, in_specs=placed, out_specs=P("wide", "narrow"), check_vma=False,
    )
```

time: 1150 us -> 42.1 us (0.04)
  blocking collectives: 1080 us -> 0 us
  Pallas kernels: 0 us -> 40.7 us
  waiting for transfers between devices: 24.9 us -> 0 us
  between operations: 14.2 us -> 0.01 us
  local copies, waits for them, and re-layouts: 14.5 us -> 1.28 us
    unnamed x1 -> x0, blocking collectives: 491 us -> none
    pmax x1 -> x0, blocking collectives: 488 us -> none  [body(): best = lax.pmax(max_table, 'wide')]
    all_gather x2 -> x0, blocking collectives: 104 us -> none  [the longest x1 93.3 us: body(): all_queries = lax.all_gather(own_queries, 'wide', axis=0, tiled=True)]
    pallas_call x0 -> x1, Pallas kernels: none -> 40.7 us  [body(): pl.pallas_call(functools.partial(layer_kernel, wide, narrow, offs), out_s...]
    reduce_scatter x2 -> x0, waiting for transfers between devices: 24.8 us -> none  [the longest x1 24.8 us: body(): lax.psum_scatter(partial_out, 'narrow', scatter_dimension=1, tiled=True)]
  transfers between devices with their start and end apart: 2 -> 0, of which waited for: 1 -> 0; matrix products, arithmetic and copies ran while one was open for 0% -> 0% of each run, Pallas kernels for 0% -> 0%
where the time goes in v1:
time: 42.1 us; the launch traced here: 42 us
  Pallas kernels  40.7 us (97%)
  local copies, waits for them, and re-layouts  1.28 us (3%)
    pallas_call x1, Pallas kernels, body(): pl.pallas_call(functools.partial(layer_kernel, wide, narrow, offs), out_s...  40.7 us
    unnamed x1, local copies, waits for them, and re-layouts  1.28 us

profile of v1, /device:TPU:1, one launch (start us, length us, event | category | flops | bytes accessed | tf_op | source)
XLA Modules:
  0.0 42.0 jit_solution(15099590143581748957)
XLA Ops:
  0.0 40.7 %shard_map.82 = bf16[8,256]{1,0:T(8,128)(2,1)} custom-call(bf16[8,256]{1,0:T(8,128)(2,1)} %tok.1, f32[1,1024]{1,0:T(1,128)} %bitcast.3, bf16[1024,2,256]{2,1,0:T(2,128)(2,1)} %wqk.1, bf16[1024,256]{1,0:T(8,128)(2,1)} %wv.1, bf16[256,1024]{1,0:T(8,128)(2,1)} %wo.1, bf16[64,2,32,256]{3,2,1,0:T(8,128)(2,1)} %kv.1, s32[1024]{0:T(1024)} %clen.1, s32[8,1024]{1,0:T(8,128)} %bitcast.2), custom_call_target="tpu_custom_call" | custom-call | tf_op jit(solution)/shard_map/pallas_call | solution.py:246
  40.7 1.3 %copy.10 = bf16[8,256]{1,0:T(8,128)(2,1)} copy(bf16[8,256]{1,0:T(8,128)(2,1)} %shard_map.82) | data formatting | bytes 8192

commit v2 on v1

--- a/solution.py
+++ b/solution.py
@@ -13,24 +13,20 @@
 
 
 def layer_kernel(
-    wide, narrow, offs,
+    wide, narrow, stride_len,
     tok, gain, wqk, wv, wo, kv, clen, ptab, out,
     tokb, gainb, wqkb, wvb, wob, kvb, lenb, ptb, qin, pout, pin, rsout, rsin,
-    lsem, tsend, trecv, qsend, qrecv, psend, precv, rsend, rrecv,
+    lsem, tsend, trecv, qsend, qrecv, psend, precv, rsend, rrecv, esem,
 ):
     me_w = lax.axis_index("wide")
     me_x = lax.axis_index("narrow")
     tcount, width = tok.shape
-    pages = len(offs)
+    pages = ptab.shape[0]
+    offs = tuple((j - j % 2) * stride_len + j % 2 for j in range(pages))
+    direct, relayed, answer_order = (1, 2, 3, 6, 7), (4, 5), (2, 3, 6, 7, 1)
     heads = width // HEAD_DIM
     page_len = kvb.shape[2]
     span = tcount * page_len
-
-    def fwd(j):
-        return lax.rem(me_w + offs[j], wide)
-
-    def bwd(j):
-        return lax.rem(me_w + (wide - offs[j]), wide)
 
     local = [
         pltpu.make_async_copy(tok, tokb.at[me_x], lsem.at[0]),
@@ -42,21 +38,31 @@
         pltpu.make_async_copy(kv, kvb, lsem.at[6]),
         pltpu.make_async_copy(wo, wob, lsem.at[7]),
     ]
+
+    barrier = pltpu.get_barrier_semaphore()
+
+    def greet(target):
+        pl.semaphore_signal(barrier, inc=1, device_id=target, device_id_type=MESH)
+
+    expected = narrow - 1
+    for d in range(1, narrow):
+        greet((me_w, lax.rem(me_x + d, narrow)))
+    for j in direct:
+        pl.when(me_w + offs[j] < wide)(lambda j=j: greet((me_w + offs[j], me_x)))
+        pl.when(me_w < offs[j])(lambda j=j: greet((me_w + wide - offs[j], me_x)))
+        expected = expected + (me_w + wide - offs[j]) // wide + (me_w + offs[j]) // wide
+    for j in relayed:
+        pl.when(me_w < offs[j])(lambda j=j: greet((me_w + wide - offs[j], me_x)))
+        expected = expected + (me_w + offs[j]) // wide
     for copy in local:
         copy.start()
-
-    around = sorted({o for o in offs if o} | {wide - o for o in offs if o})
-    barrier = pltpu.get_barrier_semaphore()
-    for d in range(1, narrow):
-        pl.semaphore_signal(
-            barrier, inc=1, device_id=(me_w, lax.rem(me_x + d, narrow)), device_id_type=MESH
-        )
-    for o in around:
-        pl.semaphore_signal(
-            barrier, inc=1, device_id=(lax.rem(me_w + o, wide), me_x), device_id_type=MESH
-        )
-    pl.semaphore_wait(barrier, narrow - 1 + len(around))
-
+    pl.semaphore_wait(barrier, expected)
+    for j in answer_order:
+        pl.when(me_w >= offs[j])(
+            lambda j=j: pl.semaphore_signal(
+                esem.at[j], inc=1, device_id=(me_w - offs[j], me_x), device_id_type=MESH
+            )
+        )
     tcopies = [
         pltpu.make_async_remote_copy(
             src_ref=tok, dst_ref=tokb.at[me_x], send_sem=tsend.at[d - 1], recv_sem=trecv.at[d - 1],
@@ -64,8 +70,8 @@
         )
         for d in range(1, narrow)
     ]
-    for copy in tcopies:
-        copy.start()
+    for d in range(1, narrow):
+        tcopies[d - 1].start()
     local[0].wait()
     local[1].wait()
     for copy in tcopies:
@@ -97,21 +103,30 @@
 
     query = project(lambda a, b: wqkb[a:b, 0, :])
     qin[0] = query
-    qcopies = {
-        j: pltpu.make_async_remote_copy(
-            src_ref=qin.at[0], dst_ref=qin.at[j], send_sem=qsend.at[j], recv_sem=qrecv.at[j],
-            device_id=(fwd(j), me_x), device_id_type=MESH,
-        )
-        for j in range(1, pages)
-    }
-    far = sorted(range(1, pages), key=lambda j: -min(offs[j], wide - offs[j]))
-    for j in far:
-        qcopies[j].start()
-
-    new_keys = project(lambda a, b: wqkb[a:b, 1, :]).astype(jnp.float32)
-    local[3].wait()
-    new_values = project(lambda a, b: wvb[a:b, :]).astype(jnp.float32)
-    products = query.astype(jnp.float32) * new_keys
+
+    def query_copy(source, o, j):
+        return pltpu.make_async_remote_copy(
+            src_ref=qin.at[source], dst_ref=qin.at[j], send_sem=qsend.at[j], recv_sem=qrecv.at[j],
+            device_id=(lax.rem(me_w + o, wide), me_x), device_id_type=MESH,
+        )
+
+    qcopies = {j: query_copy(0, offs[j], j) for j in direct + relayed}
+    relays = {j: query_copy(2, offs[j] - offs[2], j) for j in relayed}
+
+    def known(j):
+        pl.when(me_w + offs[j] >= wide)(qcopies[j].start)
+
+    def unknown(j):
+        @pl.when(me_w + offs[j] < wide)
+        def _():
+            pl.semaphore_wait(esem.at[j], 1)
+            qcopies[j].start()
+
+    for j in relayed + direct:
+        known(j)
+    for j in (1, 2, 3):
+        unknown(j)
+
     lane = lax.broadcasted_iota(jnp.int32, (tcount, 128), 1)
     head_of = lax.broadcasted_iota(jnp.int32, (tcount, width), 1) // HEAD_DIM
 
@@ -121,22 +136,17 @@
             tile = jnp.where(lane == base + h, column, tile)
         return tile
 
-    self_score = stat_tile(
-        [
-            jnp.sum(jnp.where(head_of == h, products, 0.0), axis=-1, keepdims=True)
-            for h in range(heads)
-        ],
-        0, jnp.full((tcount, 128), NEG, jnp.float32),
-    )
-
     local[4].wait()
     local[5].wait()
     local[6].wait()
     row = lax.broadcasted_iota(jnp.int32, (tcount, span), 0)
     place = lax.broadcasted_iota(jnp.int32, (tcount, span), 1) - row * page_len
 
+    def offset(j):
+        return (j - j % 2) * stride_len + j % 2
+
     def attend(j):
-        home = bwd(j) * tcount
+        home = lax.rem(me_w + (wide - offset(j)), wide) * tcount
         q = qin[j].astype(jnp.float32)
         spread = jnp.concatenate(
             [jnp.where(head_of == h, q, 0.0) for h in range(heads)], axis=0
@@ -171,25 +181,66 @@
         )
         return mine, stats
 
-    pcopies = {
-        j: pltpu.make_async_remote_copy(
+    def partial_copy(j):
+        return pltpu.make_async_remote_copy(
             src_ref=pout.at[j], dst_ref=pin.at[j], send_sem=psend.at[j], recv_sem=precv.at[j],
-            device_id=(bwd(j), me_x), device_id_type=MESH,
-        )
-        for j in range(1, pages)
-    }
-    mine, stats = attend(0)
-    pin[0, :, :width] = mine
-    pin[0, :, width:] = stats
-    for j in reversed(far):
-        qcopies[j].wait_recv()
-        mine, stats = attend(j)
-        pout[j, :, :width] = mine
-        pout[j, :, width:] = stats
-        pcopies[j].start()
-
-    for j in reversed(far):
-        pcopies[j].wait_recv()
+            device_id=(lax.rem(me_w + (wide - offset(j)), wide), me_x), device_id_type=MESH,
+        )
+
+    def keep(ref, j, result):
+        ref[j, :, :width] = result[0]
+        ref[j, :, width:] = result[1]
+
+    for j in direct[3:]:
+        unknown(j)
+
+    first = (wide - me_w) // wide
+
+    def turn_of(turn, part):
+        return (turn + 3) // 4 * (1 + ((turn + 2) * (1 + part % 2) + 2 * ((3 - part) // 3)) % 3)
+
+    def pair(step, carry):
+        turn = (step + first) % 4
+        even = 2 * turn_of(turn, me_w * 4 // wide)
+        odd = 2 * turn_of(turn, (me_w + first - 1) * 4 // wide) + 1
+
+        @pl.when(turn == 0)
+        def _():
+            qcopies[1].wait_recv()
+            keep(pout, 1, attend(1))
+            partial_copy(1).start()
+
+        @pl.when(turn > 0)
+        def _():
+            query_copy(0, offs[2], even).wait_recv()
+            for j in relayed:
+                pl.when((even == 2) & (me_w >= offs[2]) & (me_w < wide + offs[2] - offs[j]))(
+                    relays[j].start
+                )
+            query_copy(0, offs[2], odd).wait_recv()
+            results = attend(even), attend(odd)
+            keep(pout, even, results[0])
+            partial_copy(even).start()
+            keep(pout, odd, results[1])
+            partial_copy(odd).start()
+
+        return carry
+
+    lax.fori_loop(0, pages // 2, pair, 0)
+    keep(pin, 0, attend(0))
+    new_keys = project(lambda a, b: wqkb[a:b, 1, :]).astype(jnp.float32)
+    local[3].wait()
+    new_values = project(lambda a, b: wvb[a:b, :]).astype(jnp.float32)
+    products = query.astype(jnp.float32) * new_keys
+    self_score = stat_tile(
+        [
+            jnp.sum(jnp.where(head_of == h, products, 0.0), axis=-1, keepdims=True)
+            for h in range(heads)
+        ],
+        0, jnp.full((tcount, 128), NEG, jnp.float32),
+    )
+    for j in range(1, pages):
+        partial_copy(j).wait_recv()
 
     stats = [pin[j, :, width:] for j in range(pages)]
     best = functools.reduce(jnp.maximum, stats, self_score)
@@ -231,8 +282,13 @@
         rcopies[d - 1].wait_recv()
         total = total + rsin[d - 1]
     out[...] = total.astype(out.dtype)
-    for copy in tcopies + rcopies + [qcopies[j] for j in far] + [pcopies[j] for j in far]:
+    for copy in tcopies + rcopies + [partial_copy(j) for j in range(1, pages)]:
         copy.wait_send()
+    for j in direct:
+        qcopies[j].wait_send()
+    for j in relayed:
+        pl.when(me_w + offs[j] >= wide)(qcopies[j].wait_send)
+        pl.when((me_w >= offs[2]) & (me_w < wide + offs[2] - offs[j]))(relays[j].wait_send)
 
 
 def body(wide, narrow, tokens, norm_gain, w_qk, w_value, w_out, kv_cache, cache_len, page_table):
@@ -240,11 +296,10 @@
     total, pages = page_table.shape
     features = norm_gain.shape[0]
     stride_len = wide // pages
-    offs = tuple(((j - j % 2) * stride_len + j % 2) % wide for j in range(pages))
-    anywhere = pl.BlockSpec(memory_space=pl.ANY)
+    anywhere = pl.BlockSpec(memory_space=pltpu.HBM)
     dma = pltpu.SemaphoreType.DMA
     return pl.pallas_call(
-        functools.partial(layer_kernel, wide, narrow, offs),
+        functools.partial(layer_kernel, wide, narrow, stride_len),
         out_shape=jax.ShapeDtypeStruct((tcount, width), jnp.bfloat16),
         in_specs=[anywhere] * 8,
         out_specs=pl.BlockSpec(memory_space=pltpu.VMEM),
@@ -267,6 +322,7 @@
             dma((pages,)), dma((pages,)),
             dma((pages,)), dma((pages,)),
             dma((narrow - 1,)), dma((narrow - 1,)),
+            pltpu.SemaphoreType.REGULAR((pages,)),
         ],
         compiler_params=pltpu.CompilerParams(
             collective_id=0, has_side_effects=True, vmem_limit_bytes=62 << 20

time: 42.1 us -> 38.3 us (0.910)
  the two profiles are of different devices: /device:TPU:1 before, /device:TPU:2 now
where the time goes in v2:
time: 38.3 us; the launch traced here: 38.1 us
  Pallas kernels  36.9 us (96%)
  local copies, waits for them, and re-layouts  1.28 us (3%)
    pallas_call x1, Pallas kernels, body(): pl.pallas_call(functools.partial(layer_kernel, wide, narrow, stride_len),...  36.9 us
    unnamed x1, local copies, waits for them, and re-layouts  1.28 us

profile of v2, /device:TPU:2, one launch (start us, length us, event | category | flops | bytes accessed | tf_op | source)
XLA Modules:
  0.0 38.1 jit_solution(3172393755290763396)
XLA Ops:
  0.0 36.9 %shard_map.82 = bf16[8,256]{1,0:T(8,128)(2,1)} custom-call(bf16[8,256]{1,0:T(8,128)(2,1)} %tok.1, f32[1,1024]{1,0:T(1,128)} %bitcast.3, bf16[1024,2,256]{2,1,0:T(2,128)(2,1)} %wqk.1, bf16[1024,256]{1,0:T(8,128)(2,1)} %wv.1, bf16[256,1024]{1,0:T(8,128)(2,1)} %wo.1, bf16[64,2,32,256]{3,2,1,0:T(8,128)(2,1)} %kv.1, s32[1024]{0:T(1024)} %clen.1, s32[8,1024]{1,0:T(8,128)} %bitcast.2), custom_call_target="tpu_custom_call" | custom-call | tf_op jit(solution)/shard_map/pallas_call | solution.py:301
  36.9 1.3 %copy.10 = bf16[8,256]{1,0:T(8,128)(2,1)} copy(bf16[8,256]{1,0:T(8,128)(2,1)} %shard_map.82) | data formatting | bytes 8192

commit v3 on v2

--- a/solution.py
+++ b/solution.py
@@ -9,14 +9,20 @@
 
 HEAD_DIM = 64
 MESH = pl.DeviceIdType.MESH
+ORDERS = (
+    ((1, 6, 7, 2, 3, 4, 5), (1, 6, 7, 2, 3, 4, 5), (6, 7, 2, 3, 4, 5, 1)),
+    ((1, 2, 3, 6, 7, 4, 5), (1, 2, 3, 6, 7, 4, 5), (1, 2, 7, 6, 3, 4, 5)),
+    ((4, 5, 1, 2, 3, 6, 7), (4, 2, 1, 5, 3, 6, 7), (4, 2, 3, 1, 7, 6, 5)),
+    ((1, 2, 3, 6, 7, 4, 5), (2, 6, 1, 3, 7, 4, 5), (2, 6, 4, 3, 5, 1, 7)),
+)
 NEG = -1e30
 
 
 def layer_kernel(
-    wide, narrow, stride_len,
+    wide, narrow, stride_len, row_len,
     tok, gain, wqk, wv, wo, kv, clen, ptab, out,
-    tokb, gainb, wqkb, wvb, wob, kvb, lenb, ptb, qin, pout, pin, rsout, rsin,
-    lsem, tsend, trecv, qsend, qrecv, psend, precv, rsend, rrecv, esem,
+    tokb, gainb, wqkb, wqb, wvb, wob, kvb, lenb, ptb, qin, pout, pin, rsout, rsin,
+    lsem, tsend, trecv, qsend, qrecv, psend, precv, rsend, rrecv, esem, outb,
 ):
     me_w = lax.axis_index("wide")
     me_x = lax.axis_index("narrow")
@@ -47,32 +53,41 @@
     expected = narrow - 1
     for d in range(1, narrow):
         greet((me_w, lax.rem(me_x + d, narrow)))
-    for j in direct:
+    for j in direct[1:]:
         pl.when(me_w + offs[j] < wide)(lambda j=j: greet((me_w + offs[j], me_x)))
         pl.when(me_w < offs[j])(lambda j=j: greet((me_w + wide - offs[j], me_x)))
         expected = expected + (me_w + wide - offs[j]) // wide + (me_w + offs[j]) // wide
     for j in relayed:
         pl.when(me_w < offs[j])(lambda j=j: greet((me_w + wide - offs[j], me_x)))
         expected = expected + (me_w + offs[j]) // wide
+    ahead, behind = lax.rem(me_w + 1, wide), lax.rem(me_w + wide - 1, wide)
+    in_row = lax.rem(me_w, row_len)
+    led = in_row // (row_len - 1) * (me_w // (wide // 2))
+    leads = (1 - (in_row + row_len - 1) // row_len) * (behind // (wide // 2))
+    pl.when(led == 0)(lambda: greet((ahead, me_x)))
+    pl.when(leads == 1)(lambda: greet((behind, me_x)))
+    expected = expected + 1 - leads + led
     for copy in local:
         copy.start()
     pl.semaphore_wait(barrier, expected)
     for j in answer_order:
-        pl.when(me_w >= offs[j])(
+        pl.when(me_w >= offs[j] if j > 1 else leads == 0)(
             lambda j=j: pl.semaphore_signal(
                 esem.at[j], inc=1, device_id=(me_w - offs[j], me_x), device_id_type=MESH
             )
         )
     tcopies = [
         pltpu.make_async_remote_copy(
-            src_ref=tok, dst_ref=tokb.at[me_x], send_sem=tsend.at[d - 1], recv_sem=trecv.at[d - 1],
+            src_ref=tokb.at[me_x], dst_ref=tokb.at[me_x], send_sem=tsend.at[d - 1], recv_sem=trecv.at[d - 1],
             device_id=(me_w, lax.rem(me_x + d, narrow)), device_id_type=MESH,
         )
         for d in range(1, narrow)
     ]
-    for d in range(1, narrow):
-        tcopies[d - 1].start()
     local[0].wait()
+    for copy in tcopies:
+        copy.start()
+    local[2].wait()
+    wqb[...] = wqkb[:, 0, :]
     local[1].wait()
     for copy in tcopies:
         copy.wait_recv()
@@ -86,8 +101,6 @@
         (floats[i] * scale * gainb[:, i * width:(i + 1) * width]).astype(jnp.bfloat16)
         for i in range(narrow)
     ]
-
-    local[2].wait()
 
     def project(weight):
         return functools.reduce(
@@ -101,7 +114,7 @@
             ],
         ).astype(jnp.bfloat16)
 
-    query = project(lambda a, b: wqkb[a:b, 0, :])
+    query = project(lambda a, b: wqb[a:b])
     qin[0] = query
 
     def query_copy(source, o, j):
@@ -114,10 +127,10 @@
     relays = {j: query_copy(2, offs[j] - offs[2], j) for j in relayed}
 
     def known(j):
-        pl.when(me_w + offs[j] >= wide)(qcopies[j].start)
+        pl.when(me_w + offs[j] >= wide if j > 1 else led == 1)(qcopies[j].start)
 
     def unknown(j):
-        @pl.when(me_w + offs[j] < wide)
+        @pl.when(me_w + offs[j] < wide if j > 1 else led == 0)
         def _():
             pl.semaphore_wait(esem.at[j], 1)
             qcopies[j].start()
@@ -194,39 +207,34 @@
     for j in direct[3:]:
         unknown(j)
 
-    first = (wide - me_w) // wide
-
-    def turn_of(turn, part):
-        return (turn + 3) // 4 * (1 + ((turn + 2) * (1 + part % 2) + 2 * ((3 - part) // 3)) % 3)
-
-    def pair(step, carry):
-        turn = (step + first) % 4
-        even = 2 * turn_of(turn, me_w * 4 // wide)
-        odd = 2 * turn_of(turn, (me_w + first - 1) * 4 // wide) + 1
-
-        @pl.when(turn == 0)
-        def _():
-            qcopies[1].wait_recv()
-            keep(pout, 1, attend(1))
-            partial_copy(1).start()
-
-        @pl.when(turn > 0)
-        def _():
-            query_copy(0, offs[2], even).wait_recv()
-            for j in relayed:
-                pl.when((even == 2) & (me_w >= offs[2]) & (me_w < wide + offs[2] - offs[j]))(
-                    relays[j].start
-                )
-            query_copy(0, offs[2], odd).wait_recv()
-            results = attend(even), attend(odd)
-            keep(pout, even, results[0])
-            partial_copy(even).start()
-            keep(pout, odd, results[1])
-            partial_copy(odd).start()
-
-        return carry
-
-    lax.fori_loop(0, pages // 2, pair, 0)
+    relay = (me_w + wide - offs[2]) // wide * ((2 * wide + offs[2] - offs[4] - 1 - me_w) // wide)
+
+    @pl.when(relay > 0)
+    def _():
+        qcopies[2].wait_recv()
+        relays[4].start()
+        pl.when(me_w < wide + offs[2] - offs[5])(relays[5].start)
+
+    def digits(order):
+        return sum(j * 8**at for at, j in enumerate(order))
+
+    part, quarter = me_w * 4 // wide, wide // 4
+    row_first = 1 - (in_row + row_len - 1) // row_len
+    part_first = 1 - (lax.rem(me_w, quarter) + quarter - 1) // quarter
+    code = 0
+    for at, orders in enumerate(ORDERS):
+        inside, start, edge = (digits(order) for order in orders)
+        here = 1 - (lax.rem(part - at + 4, 4) + 3) // 4
+        code = code + here * (inside + row_first * (start - inside) + part_first * (edge - start))
+
+    def page(step, code):
+        j = lax.rem(code, 8)
+        pl.when((j != 2) | (relay == 0))(query_copy(0, offs[2], j).wait_recv)
+        keep(pout, j, attend(j))
+        partial_copy(j).start()
+        return code // 8
+
+    lax.fori_loop(0, pages - 1, page, code)
     keep(pin, 0, attend(0))
     new_keys = project(lambda a, b: wqkb[a:b, 1, :]).astype(jnp.float32)
     local[3].wait()
@@ -281,14 +289,17 @@
     for d in range(1, narrow):
         rcopies[d - 1].wait_recv()
         total = total + rsin[d - 1]
-    out[...] = total.astype(out.dtype)
+    outb[...] = total.astype(out.dtype)
+    last = pltpu.make_async_copy(outb, out, lsem.at[0])
+    last.start()
+    last.wait()
     for copy in tcopies + rcopies + [partial_copy(j) for j in range(1, pages)]:
         copy.wait_send()
     for j in direct:
         qcopies[j].wait_send()
     for j in relayed:
         pl.when(me_w + offs[j] >= wide)(qcopies[j].wait_send)
-        pl.when((me_w >= offs[2]) & (me_w < wide + offs[2] - offs[j]))(relays[j].wait_send)
+        pl.when((relay > 0) & (me_w < wide + offs[2] - offs[j]))(relays[j].wait_send)
 
 
 def body(wide, narrow, tokens, norm_gain, w_qk, w_value, w_out, kv_cache, cache_len, page_table):
@@ -299,14 +310,15 @@
     anywhere = pl.BlockSpec(memory_space=pltpu.HBM)
     dma = pltpu.SemaphoreType.DMA
     return pl.pallas_call(
-        functools.partial(layer_kernel, wide, narrow, stride_len),
+        functools.partial(layer_kernel, wide, narrow, stride_len, wide // 16),
         out_shape=jax.ShapeDtypeStruct((tcount, width), jnp.bfloat16),
         in_specs=[anywhere] * 8,
-        out_specs=pl.BlockSpec(memory_space=pltpu.VMEM),
+        out_specs=pl.BlockSpec(memory_space=pl.ANY),
         scratch_shapes=[
             pltpu.VMEM((narrow, tcount, width), jnp.bfloat16),
             pltpu.VMEM((1, features), jnp.float32),
             pltpu.VMEM(w_qk.shape, jnp.bfloat16),
+            pltpu.VMEM((features, width), jnp.bfloat16),
             pltpu.VMEM(w_value.shape, jnp.bfloat16),
             pltpu.VMEM(w_out.shape, jnp.bfloat16),
             pltpu.VMEM(kv_cache.shape, jnp.bfloat16),
@@ -323,6 +335,7 @@
             dma((pages,)), dma((pages,)),
             dma((narrow - 1,)), dma((narrow - 1,)),
             pltpu.SemaphoreType.REGULAR((pages,)),
+            pltpu.VMEM((tcount, width), jnp.bfloat16),
         ],
         compiler_params=pltpu.CompilerParams(
             collective_id=0, has_side_effects=True, vmem_limit_bytes=62 << 20

time: 38.3 us -> 36.1 us (0.943)
  the two profiles are of different devices: /device:TPU:2 before, /device:TPU:1 now
where the time goes in v3:
time: 36.1 us; the launch traced here: 35.5 us
  Pallas kernels  34.2 us (95%)
  local copies, waits for them, and re-layouts  1.28 us (4%)
    pallas_call x1, Pallas kernels, body(): pl.pallas_call(functools.partial(layer_kernel, wide, narrow, stride_len,...  34.2 us
    unnamed x1, local copies, waits for them, and re-layouts  1.28 us

profile of v3, /device:TPU:1, one launch (start us, length us, event | category | flops | bytes accessed | tf_op | source)
XLA Modules:
  0.0 35.5 jit_solution(4521512725407112204)
XLA Ops:
  0.0 34.2 %shard_map.82 = bf16[8,256]{1,0:T(8,128)(2,1)} custom-call(bf16[8,256]{1,0:T(8,128)(2,1)} %tok.1, f32[1,1024]{1,0:T(1,128)} %bitcast.3, bf16[1024,2,256]{2,1,0:T(2,128)(2,1)} %wqk.1, bf16[1024,256]{1,0:T(8,128)(2,1)} %wv.1, bf16[256,1024]{1,0:T(8,128)(2,1)} %wo.1, bf16[64,2,32,256]{3,2,1,0:T(8,128)(2,1)} %kv.1, s32[1024]{0:T(1024)} %clen.1, s32[8,1024]{1,0:T(8,128)} %bitcast.2), custom_call_target="tpu_custom_call" | custom-call | tf_op jit(solution)/shard_map/pallas_call | solution.py:312
  34.3 1.3 %copy.10 = bf16[8,256]{1,0:T(8,128)(2,1)} copy(bf16[8,256]{1,0:T(8,128)(2,1)} %shard_map.82) | data formatting | bytes 8192

commit v4 on v3

--- a/solution.py
+++ b/solution.py
@@ -12,8 +12,8 @@
 ORDERS = (
     ((1, 6, 7, 2, 3, 4, 5), (1, 6, 7, 2, 3, 4, 5), (6, 7, 2, 3, 4, 5, 1)),
     ((1, 2, 3, 6, 7, 4, 5), (1, 2, 3, 6, 7, 4, 5), (1, 2, 7, 6, 3, 4, 5)),
-    ((4, 5, 1, 2, 3, 6, 7), (4, 2, 1, 5, 3, 6, 7), (4, 2, 3, 1, 7, 6, 5)),
-    ((1, 2, 3, 6, 7, 4, 5), (2, 6, 1, 3, 7, 4, 5), (2, 6, 4, 3, 5, 1, 7)),
+    ((4, 5, 2, 3, 1, 6, 7), (4, 2, 5, 3, 1, 6, 7), (4, 2, 3, 1, 7, 6, 5)),
+    ((6, 7, 1, 4, 5, 2, 3), (6, 1, 4, 7, 5, 2, 3), (6, 4, 3, 5, 2, 1, 7)),
 )
 NEG = -1e30
 
@@ -21,8 +21,8 @@
 def layer_kernel(
     wide, narrow, stride_len, row_len,
     tok, gain, wqk, wv, wo, kv, clen, ptab, out,
-    tokb, gainb, wqkb, wqb, wvb, wob, kvb, lenb, ptb, qin, pout, pin, rsout, rsin,
-    lsem, tsend, trecv, qsend, qrecv, psend, precv, rsend, rrecv, esem, outb,
+    tokb, gainb, wqkb, wqb, wvb, wob, kvb, lenb, ptb, qin, pout, pin, rsout,
+    lsem, tsend, trecv, qsend, qrecv, psend, precv, rsend, rrecv, esem,
 ):
     me_w = lax.axis_index("wide")
     me_x = lax.axis_index("narrow")
@@ -83,9 +83,10 @@
         )
         for d in range(1, narrow)
     ]
+    far_first = sorted(range(1, narrow), key=lambda d: -min(d, narrow - d))
     local[0].wait()
-    for copy in tcopies:
-        copy.start()
+    for d in far_first:
+        tcopies[d - 1].start()
     local[2].wait()
     wqb[...] = wqkb[:, 0, :]
     local[1].wait()
@@ -124,7 +125,15 @@
         )
 
     qcopies = {j: query_copy(0, offs[j], j) for j in direct + relayed}
-    relays = {j: query_copy(2, offs[j] - offs[2], j) for j in relayed}
+    quarter = wide // 4
+    relay = (wide - 1 - me_w) // (2 * quarter)
+    back = relay * (1 - me_w // quarter)
+    source = 2 + 4 * back
+    relays = {
+        4: query_copy(source, offs[2] + back * (offs[6] - offs[2]), 4),
+        5: query_copy(source, offs[3] + back * (offs[7] - offs[3]), 5),
+    }
+    relay_odd = (relay > 0) & (me_w != quarter - 1)
 
     def known(j):
         pl.when(me_w + offs[j] >= wide if j > 1 else led == 1)(qcopies[j].start)
@@ -207,18 +216,16 @@
     for j in direct[3:]:
         unknown(j)
 
-    relay = (me_w + wide - offs[2]) // wide * ((2 * wide + offs[2] - offs[4] - 1 - me_w) // wide)
-
     @pl.when(relay > 0)
     def _():
-        qcopies[2].wait_recv()
+        query_copy(0, offs[2], source).wait_recv()
         relays[4].start()
-        pl.when(me_w < wide + offs[2] - offs[5])(relays[5].start)
+        pl.when(relay_odd)(relays[5].start)
 
     def digits(order):
         return sum(j * 8**at for at, j in enumerate(order))
 
-    part, quarter = me_w * 4 // wide, wide // 4
+    part = me_w // quarter
     row_first = 1 - (in_row + row_len - 1) // row_len
     part_first = 1 - (lax.rem(me_w, quarter) + quarter - 1) // quarter
     code = 0
@@ -229,7 +236,7 @@
 
     def page(step, code):
         j = lax.rem(code, 8)
-        pl.when((j != 2) | (relay == 0))(query_copy(0, offs[2], j).wait_recv)
+        pl.when((j != source) | (relay == 0))(query_copy(0, offs[2], j).wait_recv)
         keep(pout, j, attend(j))
         partial_copy(j).start()
         return code // 8
@@ -271,35 +278,36 @@
 
     local[7].wait()
     rcopies = []
-    for d in range(1, narrow):
+    for d in far_first:
         peer = lax.rem(me_x + d, narrow)
         start = pl.multiple_of(peer * width, width)
         rsout[d - 1] = jnp.dot(
             heads_out, wob[:, pl.ds(start, width)], preferred_element_type=jnp.float32
         )
         copy = pltpu.make_async_remote_copy(
-            src_ref=rsout.at[d - 1], dst_ref=rsin.at[d - 1],
+            src_ref=rsout.at[d - 1], dst_ref=out.at[d - 1],
             send_sem=rsend.at[d - 1], recv_sem=rrecv.at[d - 1],
             device_id=(me_w, peer), device_id_type=MESH,
         )
         copy.start()
         rcopies.append(copy)
     start = pl.multiple_of(me_x * width, width)
-    total = jnp.dot(heads_out, wob[:, pl.ds(start, width)], preferred_element_type=jnp.float32)
-    for d in range(1, narrow):
-        rcopies[d - 1].wait_recv()
-        total = total + rsin[d - 1]
-    outb[...] = total.astype(out.dtype)
-    last = pltpu.make_async_copy(outb, out, lsem.at[0])
-    last.start()
-    last.wait()
-    for copy in tcopies + rcopies + [partial_copy(j) for j in range(1, pages)]:
+    rsout[narrow - 1] = jnp.dot(
+        heads_out, wob[:, pl.ds(start, width)], preferred_element_type=jnp.float32
+    )
+    own = pltpu.make_async_copy(rsout.at[narrow - 1], out.at[narrow - 1], lsem.at[0])
+    own.start()
+    for copy in tcopies + [partial_copy(j) for j in range(1, pages)]:
         copy.wait_send()
     for j in direct:
         qcopies[j].wait_send()
     for j in relayed:
         pl.when(me_w + offs[j] >= wide)(qcopies[j].wait_send)
-        pl.when((relay > 0) & (me_w < wide + offs[2] - offs[j]))(relays[j].wait_send)
+    pl.when(relay > 0)(relays[4].wait_send)
+    pl.when(relay_odd)(relays[5].wait_send)
+    own.wait()
+    for copy in rcopies:
+        copy.wait()
 
 
 def body(wide, narrow, tokens, norm_gain, w_qk, w_value, w_out, kv_cache, cache_len, page_table):
@@ -309,9 +317,9 @@
     stride_len = wide // pages
     anywhere = pl.BlockSpec(memory_space=pltpu.HBM)
     dma = pltpu.SemaphoreType.DMA
-    return pl.pallas_call(
+    sums = pl.pallas_call(
         functools.partial(layer_kernel, wide, narrow, stride_len, wide // 16),
-        out_shape=jax.ShapeDtypeStruct((tcount, width), jnp.bfloat16),
+        out_shape=jax.ShapeDtypeStruct((narrow, tcount, width), jnp.float32),
         in_specs=[anywhere] * 8,
         out_specs=pl.BlockSpec(memory_space=pl.ANY),
         scratch_shapes=[
@@ -327,15 +335,13 @@
             pltpu.VMEM((pages, tcount, width), jnp.bfloat16),
             pltpu.VMEM((pages, tcount, width + 128), jnp.float32),
             pltpu.VMEM((pages, tcount, width + 128), jnp.float32),
-            pltpu.VMEM((narrow - 1, tcount, width), jnp.float32),
-            pltpu.VMEM((narrow - 1, tcount, width), jnp.float32),
+            pltpu.VMEM((narrow, tcount, width), jnp.float32),
             dma((8,)),
             dma((narrow - 1,)), dma((narrow - 1,)),
             dma((pages,)), dma((pages,)),
             dma((pages,)), dma((pages,)),
             dma((narrow - 1,)), dma((narrow - 1,)),
             pltpu.SemaphoreType.REGULAR((pages,)),
-            pltpu.VMEM((tcount, width), jnp.bfloat16),
         ],
         compiler_params=pltpu.CompilerParams(
             collective_id=0, has_side_effects=True, vmem_limit_bytes=62 << 20
@@ -344,6 +350,7 @@
         tokens, norm_gain.reshape(1, features), w_qk, w_value, w_out, kv_cache, cache_len,
         page_table.T,
     )
+    return jnp.sum(sums, axis=0).astype(jnp.bfloat16)
 
 
 def solution(mesh):

time: 36.1 us -> 35 us (0.970)
  other arithmetic: 0 us -> 1.36 us
  local copies, waits for them, and re-layouts: 1.28 us -> 0 us
  Pallas kernels: 34.2 us -> 33.3 us
    reduce_sum x0 -> x1, other arithmetic: none -> 1.36 us  [body(): return jnp.sum(sums, axis=0).astype(jnp.bfloat16)]
    unnamed x1 -> x0, local copies, waits for them, and re-layouts: 1.28 us -> none
    pallas_call x1, Pallas kernels: 34.2 us -> 33.3 us  [body(): pl.pallas_call(functools.partial(layer_kernel, wide, narrow, stride_len,...]
where the time goes in v4:
time: 35 us; the launch traced here: 34.6 us
  Pallas kernels  33.3 us (95%)
  other arithmetic  1.36 us (4%)
    pallas_call x1, Pallas kernels, body(): pl.pallas_call(functools.partial(layer_kernel, wide, narrow, stride_len,...  33.3 us
    reduce_sum x1, other arithmetic, body(): return jnp.sum(sums, axis=0).astype(jnp.bfloat16)  1.36 us

profile of v4, /device:TPU:1, one launch (start us, length us, event | category | flops | bytes accessed | tf_op | source)
XLA Modules:
  0.0 34.6 jit_solution(5548810589134570020)
XLA Ops:
  0.0 33.3 %shard_map.82 = f32[4,8,256]{2,1,0:T(8,128)} custom-call(bf16[8,256]{1,0:T(8,128)(2,1)} %tok.1, f32[1,1024]{1,0:T(1,128)} %bitcast.3, bf16[1024,2,256]{2,1,0:T(2,128)(2,1)} %wqk.1, bf16[1024,256]{1,0:T(8,128)(2,1)} %wv.1, bf16[256,1024]{1,0:T(8,128)(2,1)} %wo.1, bf16[64,2,32,256]{3,2,1,0:T(8,128)(2,1)} %kv.1, s32[1024]{0:T(1024)} %clen.1, s32[8,1024]{1,0:T(8,128)} %bitcast.2), custom_call_target="tpu_custom_call" | custom-call | tf_op jit(solution)/shard_map/pallas_call | solution.py:320
  33.3 1.4 %reduce_sum.9 = bf16[8,256]{1,0:T(8,128)(2,1)} reduce(f32[4,8,256]{2,1,0:T(8,128)} %shard_map.82, f32[]{:T(128)} %constant.0.clone.1), dimensions={0}, to_apply=%region_0.0 | reduce | flops 6144 | bytes 36868 | tf_op jit(solution)/shard_map/reduce_sum | solution.py:353

commit v5 on v4

--- a/solution.py
+++ b/solution.py
@@ -22,7 +22,7 @@
     wide, narrow, stride_len, row_len,
     tok, gain, wqk, wv, wo, kv, clen, ptab, out,
     tokb, gainb, wqkb, wqb, wvb, wob, kvb, lenb, ptb, qin, pout, pin, rsout,
-    lsem, tsend, trecv, qsend, qrecv, psend, precv, rsend, rrecv, esem,
+    lsem, tsend, trecv, qsend, qrecv, psend, precv, rsend, rrecv, esem, newb, selfb,
 ):
     me_w = lax.axis_index("wide")
     me_x = lax.axis_index("narrow")
@@ -210,9 +210,32 @@
         )
 
     def keep(ref, j, result):
-        ref[j, :, :width] = result[0]
-        ref[j, :, width:] = result[1]
-
+        high = result[1].astype(jnp.bfloat16).astype(jnp.float32)
+        middle = (result[1] - high).astype(jnp.bfloat16).astype(jnp.float32)
+        terms = high + pltpu.roll(middle, 16, 1) + pltpu.roll(result[1] - high - middle, 32, 1)
+        ref[j, :, :width] = result[0].astype(jnp.bfloat16)
+        ref[j, :, width:] = terms.astype(jnp.bfloat16)
+
+    def statistics(j):
+        terms = pin[j, :, width:].astype(jnp.float32)
+        return terms + (pltpu.roll(terms, 128 - 16, 1) + pltpu.roll(terms, 128 - 32, 1))
+
+    def own_part():
+        keep(pin, 0, attend(0))
+        new_keys = project(lambda a, b: wqkb[a:b, 1, :]).astype(jnp.float32)
+        local[3].wait()
+        newb[...] = project(lambda a, b: wvb[a:b, :]).astype(jnp.float32)
+        products = query.astype(jnp.float32) * new_keys
+        selfb[...] = stat_tile(
+            [
+                jnp.sum(jnp.where(head_of == h, products, 0.0), axis=-1, keepdims=True)
+                for h in range(heads)
+            ],
+            0, jnp.full((tcount, 128), NEG, jnp.float32),
+        )
+
+    part = me_w // quarter
+    pl.when(part == 0)(own_part)
     for j in direct[3:]:
         unknown(j)
 
@@ -225,7 +248,6 @@
     def digits(order):
         return sum(j * 8**at for at, j in enumerate(order))
 
-    part = me_w // quarter
     row_first = 1 - (in_row + row_len - 1) // row_len
     part_first = 1 - (lax.rem(me_w, quarter) + quarter - 1) // quarter
     code = 0
@@ -242,22 +264,12 @@
         return code // 8
 
     lax.fori_loop(0, pages - 1, page, code)
-    keep(pin, 0, attend(0))
-    new_keys = project(lambda a, b: wqkb[a:b, 1, :]).astype(jnp.float32)
-    local[3].wait()
-    new_values = project(lambda a, b: wvb[a:b, :]).astype(jnp.float32)
-    products = query.astype(jnp.float32) * new_keys
-    self_score = stat_tile(
-        [
-            jnp.sum(jnp.where(head_of == h, products, 0.0), axis=-1, keepdims=True)
-            for h in range(heads)
-        ],
-        0, jnp.full((tcount, 128), NEG, jnp.float32),
-    )
+    pl.when(part > 0)(own_part)
     for j in range(1, pages):
         partial_copy(j).wait_recv()
 
-    stats = [pin[j, :, width:] for j in range(pages)]
+    self_score = selfb[...]
+    stats = [statistics(j) for j in range(pages)]
     best = functools.reduce(jnp.maximum, stats, self_score)
     self_factor = jnp.exp(self_score - best)
     factors = [jnp.exp(s - best) for s in stats]
@@ -271,9 +283,9 @@
             wide_tile = jnp.where(head_of == h, tile[:, h:h + 1], wide_tile)
         return wide_tile
 
-    numer = widen(self_factor) * new_values
+    numer = widen(self_factor) * newb[...]
     for j in range(pages):
-        numer = numer + widen(factors[j]) * pin[j, :, :width]
+        numer = numer + widen(factors[j]) * pin[j, :, :width].astype(jnp.float32)
     heads_out = (numer / widen(denom)).astype(jnp.bfloat16)
 
     local[7].wait()
@@ -333,8 +345,8 @@
             pltpu.SMEM((total,), jnp.int32),
             pltpu.SMEM((pages, total), jnp.int32),
             pltpu.VMEM((pages, tcount, width), jnp.bfloat16),
-            pltpu.VMEM((pages, tcount, width + 128), jnp.float32),
-            pltpu.VMEM((pages, tcount, width + 128), jnp.float32),
+            pltpu.VMEM((pages, tcount, width + 128), jnp.bfloat16),
+            pltpu.VMEM((pages, tcount, width + 128), jnp.bfloat16),
             pltpu.VMEM((narrow, tcount, width), jnp.float32),
             dma((8,)),
             dma((narrow - 1,)), dma((narrow - 1,)),
@@ -342,6 +354,8 @@
             dma((pages,)), dma((pages,)),
             dma((narrow - 1,)), dma((narrow - 1,)),
             pltpu.SemaphoreType.REGULAR((pages,)),
+            pltpu.VMEM((tcount, width), jnp.float32),
+            pltpu.VMEM((tcount, 128), jnp.float32),
         ],
         compiler_params=pltpu.CompilerParams(
             collective_id=0, has_side_effects=True, vmem_limit_bytes=62 << 20

time: 35 us -> 34.9 us (level)
  no operation moved by 1% of the time
where the time goes in v5:
time: 34.9 us; the launch traced here: 34.4 us
  Pallas kernels  33.1 us (95%)
  other arithmetic  1.36 us (4%)
    pallas_call x1, Pallas kernels, body(): pl.pallas_call(functools.partial(layer_kernel, wide, narrow, stride_len,...  33.1 us
    reduce_sum x1, other arithmetic, body(): return jnp.sum(sums, axis=0).astype(jnp.bfloat16)  1.36 us

profile of v5, /device:TPU:1, one launch (start us, length us, event | category | flops | bytes accessed | tf_op | source)
XLA Modules:
  0.0 34.4 jit_solution(13452037346968703659)
XLA Ops:
  0.0 33.1 %shard_map.82 = f32[4,8,256]{2,1,0:T(8,128)} custom-call(bf16[8,256]{1,0:T(8,128)(2,1)} %tok.1, f32[1,1024]{1,0:T(1,128)} %bitcast.3, bf16[1024,2,256]{2,1,0:T(2,128)(2,1)} %wqk.1, bf16[1024,256]{1,0:T(8,128)(2,1)} %wv.1, bf16[256,1024]{1,0:T(8,128)(2,1)} %wo.1, bf16[64,2,32,256]{3,2,1,0:T(8,128)(2,1)} %kv.1, s32[1024]{0:T(1024)} %clen.1, s32[8,1024]{1,0:T(8,128)} %bitcast.2), custom_call_target="tpu_custom_call" | custom-call | tf_op jit(solution)/shard_map/pallas_call | solution.py:332
  33.1 1.4 %reduce_sum.9 = bf16[8,256]{1,0:T(8,128)(2,1)} reduce(f32[4,8,256]{2,1,0:T(8,128)} %shard_map.82, f32[]{:T(128)} %constant.0.clone.1), dimensions={0}, to_apply=%region_0.0 | reduce | flops 6144 | bytes 36868 | tf_op jit(solution)/shard_map/reduce_sum | solution.py:367

commit v6 on v5

--- a/solution.py
+++ b/solution.py
@@ -265,27 +265,29 @@
 
     lax.fori_loop(0, pages - 1, page, code)
     pl.when(part > 0)(own_part)
-    for j in range(1, pages):
-        partial_copy(j).wait_recv()
-
-    self_score = selfb[...]
-    stats = [statistics(j) for j in range(pages)]
-    best = functools.reduce(jnp.maximum, stats, self_score)
-    self_factor = jnp.exp(self_score - best)
-    factors = [jnp.exp(s - best) for s in stats]
-    denom = self_factor
-    for j in range(pages):
-        denom = denom + factors[j] * pltpu.roll(stats[j], 64, 1)
-
     def widen(tile):
         wide_tile = jnp.zeros((tcount, width), jnp.float32)
         for h in range(heads):
             wide_tile = jnp.where(head_of == h, tile[:, h:h + 1], wide_tile)
         return wide_tile
 
-    numer = widen(self_factor) * newb[...]
-    for j in range(pages):
-        numer = numer + widen(factors[j]) * pin[j, :, :width].astype(jnp.float32)
+    def merge(js, best, denom, numer):
+        stats = [statistics(j) for j in js]
+        higher = functools.reduce(jnp.maximum, stats, best)
+        scale = jnp.exp(best - higher)
+        denom, numer = scale * denom, widen(scale) * numer
+        for j, stat in zip(js, stats):
+            factor = jnp.exp(stat - higher)
+            denom = denom + factor * pltpu.roll(stat, 64, 1)
+            numer = numer + widen(factor) * pin[j, :, :width].astype(jnp.float32)
+        return higher, denom, numer
+
+    for j in direct:
+        partial_copy(j).wait_recv()
+    merged = merge((0,) + direct, selfb[...], jnp.ones((tcount, 128), jnp.float32), newb[...])
+    for j in relayed:
+        partial_copy(j).wait_recv()
+    _, denom, numer = merge(relayed, *merged)
     heads_out = (numer / widen(denom)).astype(jnp.bfloat16)
 
     local[7].wait()

time: 34.9 us -> 34.9 us (level)
  no operation moved by 1% of the time
where the time goes in v6:
time: 34.9 us; the launch traced here: 34.4 us
  Pallas kernels  33.1 us (95%)
  other arithmetic  1.36 us (4%)
    pallas_call x1, Pallas kernels, body(): pl.pallas_call(functools.partial(layer_kernel, wide, narrow, stride_len,...  33.1 us
    reduce_sum x1, other arithmetic, body(): return jnp.sum(sums, axis=0).astype(jnp.bfloat16)  1.36 us

profile of v6, /device:TPU:1, one launch (start us, length us, event | category | flops | bytes accessed | tf_op | source)
XLA Modules:
  0.0 34.4 jit_solution(7492359200885970299)
XLA Ops:
  0.0 33.1 %shard_map.82 = f32[4,8,256]{2,1,0:T(8,128)} custom-call(bf16[8,256]{1,0:T(8,128)(2,1)} %tok.1, f32[1,1024]{1,0:T(1,128)} %bitcast.3, bf16[1024,2,256]{2,1,0:T(2,128)(2,1)} %wqk.1, bf16[1024,256]{1,0:T(8,128)(2,1)} %wv.1, bf16[256,1024]{1,0:T(8,128)(2,1)} %wo.1, bf16[64,2,32,256]{3,2,1,0:T(8,128)(2,1)} %kv.1, s32[1024]{0:T(1024)} %clen.1, s32[8,1024]{1,0:T(8,128)} %bitcast.2), custom_call_target="tpu_custom_call" | custom-call | tf_op jit(solution)/shard_map/pallas_call | solution.py:334
  33.1 1.4 %reduce_sum.9 = bf16[8,256]{1,0:T(8,128)(2,1)} reduce(f32[4,8,256]{2,1,0:T(8,128)} %shard_map.82, f32[]{:T(128)} %constant.0.clone.1), dimensions={0}, to_apply=%region_0.0 | reduce | flops 6144 | bytes 36868 | tf_op jit(solution)/shard_map/reduce_sum | solution.py:369
